TPU v7x, 256 devices: a whole 4x4x8 slice. The times are simulated.
256 devices in a mesh: ctx: 64 (over y, x, z_lo, core), grp: 4 (over z_hi).
Axes of the slice: x: 4, y: 4, z: 8 (z_hi: 4, z_lo: 2; z = z_hi * 2 + z_lo), core: 2. Of those that a mesh axis runs over, the one named last changes fastest.
Arguments:
- saved_input: bfloat16 [4, 2048, 8192], P('grp', None, 'ctx'), may hold values from -6 to 6
- out_grad: bfloat16 [4, 2048, 8192], P('grp', None, 'ctx'), may hold values from -0.0625 to 0.0625
- filters: float32 [4, 2048, 8192], P('grp', 'ctx'), may hold values from -6 to 6
- adapter_down: bfloat16 [16, 4, 2048], P(None, 'grp'), may hold values from -0.0625 to 0.0625
- adapter_up: bfloat16 [16, 4, 2048], P(None, 'grp'), may hold values from -0.25 to 0.25
Outputs:
- grad_input: bfloat16 [4, 2048, 8192], P('grp', None, 'ctx')
- grad_filter: float32 [4, 2048, 8192], P('grp', 'ctx')
- grad_down: float32 [16, 4, 2048], P(None, 'grp')
- grad_up: float32 [16, 4, 2048], P(None, 'grp')
All inputs are finite; a program needn't handle non-finite values.
Results may differ from a plain program's by a relative error of at most 0.0075.
Values may be sent and summed in bfloat16 or wider, within the bound.
A program may use at most 64 MiB of HBM per device.

v0:
```python
import functools
import math

import jax
import jax.numpy as jnp
import numpy as np
from jax import lax
from jax.experimental import pallas as pl
from jax.experimental.pallas import tpu as pltpu
from jax.sharding import PartitionSpec as P

MESH = pl.DeviceIdType.MESH
F32 = jnp.float32
BF16 = jnp.bfloat16
LANES = 128
CHANS = 32
STEP = 16
CHUNK = 16
CHUNKS = CHANS // CHUNK
SENDS = (1, 0, 1)
FILLS = (1, 1, 0)
GROUP_ORDER = (1, 2, 3)
FAR = True
DY, U, DU = 4, 4 + CHUNKS, 4 + 2 * CHUNKS
GRID = {64: (4, 4, 2, 2), 8: (2, 2, 1, 2)}
VMEM_LIMIT = 56 * 1024 * 1024
SOURCE = pl.ANY


def far_first(high, wide, direct):
    def hops(i):
        down, across = i // wide, i % wide
        return min(down, high - down) + min(across, wide - across)

    order = sorted(range(1, high * wide), key=lambda i: (-hops(i), i) if direct else i)
    late = [k for k, i in enumerate(order[:8]) if i < 8]
    if len(order) > 8:
        order.insert(7, order.pop(late[-1]))
    codes = [sum(i << (4 * k) for k, i in enumerate(part)) for part in (order[:8], order[8:])]
    return len(order), codes


def halves(table):
    high = table.astype(BF16)
    low = (table - high.astype(np.float64)).astype(BF16)
    return high, low


def make_tables(rows):
    points = 2 * rows * LANES
    n = np.arange(rows)
    p = np.arange(LANES)
    theta = np.outer(n + 0.5, n) * (2.0 * math.pi / (2 * rows))
    phi = np.outer(p, p) * (2.0 * math.pi / LANES)
    turn = np.outer(n + 0.5, p) * (2.0 * math.pi / points)
    high, low = halves(np.concatenate([np.cos(theta), -np.sin(theta)], axis=0))
    first_two = np.concatenate([high, low], axis=1)
    first_three = np.concatenate([high, high, low], axis=1)
    cos, sin = np.cos(phi), np.sin(phi)
    high, low = halves(np.block([[cos, -sin], [sin, cos]]))
    second = np.concatenate([high, high, low], axis=0)
    high, low = halves(np.block([[cos, sin], [-sin, cos]]))
    third = np.concatenate([high, high, low], axis=0)
    high, low = halves(np.concatenate([np.cos(theta).T, -np.sin(theta).T], axis=1) * (2.0 / points))
    last = np.concatenate([high, high, low], axis=1)
    twist = np.stack([np.cos(turn), np.sin(turn)]).astype(np.float32)
    return first_two, first_three, twist, second, third, last


def split(value):
    high = value.astype(BF16)
    return high, (value - high.astype(F32)).astype(BF16)


def dot(left, right, dims=((1,), (0,))):
    return lax.dot_general(left, right, (dims, ((), ())), preferred_element_type=F32)


def gather_rows(ref, first, rows):
    block = ref[:, pl.ds(pl.multiple_of(first, STEP), STEP), :].astype(F32)
    turned = jnp.swapaxes(block, 0, 1)
    return jnp.concatenate([turned[j] for j in range(STEP)], axis=1)


def forward(data, first, twist, second, exact):
    rows = data.shape[0]
    if exact:
        narrow = data.astype(BF16)
        stacked = jnp.concatenate([narrow, narrow], axis=0)
    else:
        high, low = split(data)
        stacked = jnp.concatenate([high, low, high], axis=0)
    part = dot(first[...], stacked)
    cos, sin = twist[0], twist[1]
    joined = []
    for j in range(STEP):
        lanes = slice(j * LANES, (j + 1) * LANES)
        real, imag = part[:rows, lanes], part[rows:, lanes]
        joined.append(jnp.concatenate([real * cos + imag * sin, imag * cos - real * sin], axis=1))
    high, low = split(jnp.concatenate(joined, axis=0))
    return dot(jnp.concatenate([high, low, high], axis=1), second[...])


def inverse(spectrum, twist, third, last):
    rows = twist.shape[1]
    high, low = split(spectrum)
    part = dot(jnp.concatenate([high, low, high], axis=1), third[...])
    cos, sin = twist[0], twist[1]
    reals, imags = [], []
    for j in range(STEP):
        real = part[j * rows : (j + 1) * rows, :LANES]
        imag = part[j * rows : (j + 1) * rows, LANES:]
        reals.append(real * cos - imag * sin)
        imags.append(real * sin + imag * cos)
    joined = jnp.concatenate([jnp.concatenate(reals, axis=1), jnp.concatenate(imags, axis=1)], axis=0)
    high, low = split(joined)
    return dot(last[...], jnp.concatenate([high, low, high], axis=0))


def conj_product(left, right):
    lr, li = left[:, :LANES], left[:, LANES:]
    rr, ri = right[:, :LANES], right[:, LANES:]
    return jnp.concatenate([lr * rr + li * ri, li * rr - lr * ri], axis=1)


def kernel(
    count, groups, factor,
    x_hbm, dy_hbm, h_hbm, a_hbm, b_hbm, first_two_hbm, first_three_hbm, twist_hbm, second_hbm, third_hbm, last_hbm,
    gi_ref, gf_ref, gd_ref, gu_ref,
    a_ref, b_ref, first_two, first_three, twist, second, third, last,
    x_buf, h_buf, u_buf, du_buf, dy_got, u_got, du_got, work, gf_buf,
    spec_h, spec_dy, z_mine, z_got, r_mine, r_got, parts, part_got, total, total_got,
    load_sem, send_sem, recv_sem,
):
    me = lax.axis_index("ctx")
    grp = lax.axis_index("grp")
    high, wide_x, deep, cores = GRID[count]
    core, near = me % cores, me % (deep * cores) // cores
    place = me // (deep * cores)
    down, across = place // wide_x, place % wide_x
    chips, codes = far_first(high, wide_x, FAR)
    width = count * CHANS
    ranks = a_ref.shape[0]
    inner = [
        ((near + k // cores) % deep) * cores + (core + k % cores) % cores
        for k in reversed(range(deep * cores))
    ]
    sides = [((near + k) % deep) * cores for k in reversed(range(deep))]

    def chip(t):
        code = jnp.where(t < 8, codes[0], codes[1])
        i = (code >> (4 * (t & 7))) & 15
        row = (down + i // wide_x if wide_x != 4 else down + (i >> 2)) & (high - 1)
        column = (across + i) & (wide_x - 1)
        return (row * wide_x + column) * (deep * cores)

    def each_peer(action):
        def run(t, carry):
            base = chip(t)
            for offset in inner:
                action(base + offset)
            return carry

        lax.fori_loop(0, chips, run, 0)
        for offset in inner[:-1]:
            action(place * deep * cores + offset)

    def each_owner(role, action):
        def run(t, carry):
            base = chip(t)
            for side in sides:
                action(base + side + role)
            return carry

        lax.fori_loop(0, chips, run, 0)
        for side in sides[:-1]:
            action(place * deep * cores + side + role)

        @pl.when(core != role)
        def _():
            action(place * deep * cores + sides[-1] + role)

    def each_group(action):
        for e in GROUP_ORDER:
            if e < groups:
                action(lax.rem(grp + e, groups))

    def send(src, dst, slot, target):
        pltpu.make_async_remote_copy(
            src_ref=src, dst_ref=dst, send_sem=send_sem.at[slot], recv_sem=recv_sem.at[slot],
            device_id=target, device_id_type=MESH,
        ).start()

    def wait_for(sems, slot, ref):
        pltpu.make_async_copy(ref, ref, sems.at[slot]).wait()

    def rows_of(n, size):
        return pl.ds(pl.multiple_of(n * size, size), size)

    def lanes_of(n):
        return pl.ds(pl.multiple_of(n * LANES, LANES), LANES)

    def chunk_rows(p, q):
        return pl.ds(pl.multiple_of(p * CHANS + q * CHUNK, CHUNK), CHUNK)

    barrier = pltpu.get_barrier_semaphore()

    def greet(target):
        pl.semaphore_signal(barrier, inc=1, device_id=target, device_id_type=MESH)

    each_peer(lambda p: greet({"ctx": p}))
    each_group(lambda g: greet({"grp": g}))

    loads = [
        pltpu.make_async_copy(src, dst, load_sem.at[k])
        for k, (src, dst) in enumerate(
            [
                (a_hbm, a_ref), (x_hbm, x_buf), (first_three_hbm, first_three), (twist_hbm, twist),
                (second_hbm, second), (b_hbm, b_ref), (first_two_hbm, first_two), (third_hbm, third),
                (last_hbm, last),
            ]
        )
    ]
    for load in loads:
        load.start()

    def load_h(n, carry):
        pltpu.make_async_copy(h_hbm.at[:, lanes_of(n)], h_buf.at[n], load_sem.at[9]).start()
        return carry

    lax.fori_loop(0, count, load_h, 0)
    own = [
        pltpu.make_async_copy(dy_hbm.at[chunk_rows(me, q)], dy_got.at[q, me], load_sem.at[12 + q])
        for q in range(CHUNKS)
    ]
    for copy in own:
        copy.start()
    loads[0].wait()
    loads[1].wait()
    z_mine[...] = dot(a_ref[...], x_buf[...])
    pl.semaphore_wait(barrier, count - 1 + groups - 1)

    each_group(lambda g: send(z_mine, z_got.at[grp], 0, {"grp": g}))
    for q in range(CHUNKS):
        each_peer(lambda p: send(dy_hbm.at[chunk_rows(p, q)], dy_got.at[q, me], DY + q, {"ctx": p}))

    pltpu.make_async_copy(h_buf, h_buf, load_sem.at[9]).wait()
    for load in loads[2:]:
        load.wait()

    def spectrum_h(i, carry):
        data = gather_rows(h_buf, i * STEP, count)
        spec_h[rows_of(i, STEP * count), :] = forward(data, first_three, twist, second, False)
        return carry

    lax.fori_loop(0, CHANS // STEP, spectrum_h, 0)

    def shared_sum(mine, got):
        got[grp] = mine[...]
        acc = got[0]
        for g in range(1, groups):
            acc = acc + got[g]
        return acc

    def low_rank(base, maps, value, out):
        high_part, low_part = split(value)
        pair = jnp.concatenate([high_part, low_part], axis=0)
        chunk = 256
        for start in range(0, width, chunk):
            left = maps[:, start : start + chunk]
            left = jnp.concatenate([left, left], axis=0)
            extra = dot(left, pair, ((0,), (0,)))
            out[start : start + chunk, :] = (base(start, chunk).astype(F32) + extra).astype(BF16)

    wait_for(recv_sem, 0, z_got.at[pl.ds(0, groups - 1)])
    z = shared_sum(z_mine, z_got)
    low_rank(lambda s, n: x_buf[s : s + n, :], b_ref, z, u_buf)
    for q in range(CHUNKS):
        u_got[q, me] = u_buf[chunk_rows(me, q), :]

    def send_u(q):
        each_peer(lambda p: send(u_buf.at[chunk_rows(p, q)], u_got.at[q, me], U + q, {"ctx": p}))

    pending = list(range(CHUNKS))

    def send_some(position):
        for _ in range(SENDS[position]):
            send_u(pending.pop(0))

    send_some(0)

    others = pl.ds(0, count - 1)

    def scatter_rows(ref, first, value):
        turned = jnp.stack([value[:, j * LANES : (j + 1) * LANES] for j in range(STEP)])
        ref[:, pl.ds(pl.multiple_of(first, STEP), STEP), :] = jnp.swapaxes(turned, 0, 1)

    def conv_grad(q, i, carry):
        rows = rows_of(i, STEP * count)
        spec = forward(gather_rows(dy_got.at[q], (i - q * steps) * STEP, count), first_two, twist, second, True)
        spec_dy[rows, :] = spec
        scatter_rows(work, i * STEP, inverse(conj_product(spec, spec_h[rows, :]), twist, third, last))
        return carry

    steps = CHUNK // STEP
    for q in range(CHUNKS):
        own[q].wait()
        wait_for(recv_sem, DY + q, dy_got.at[q, others])
        lax.fori_loop(q * steps, (q + 1) * steps, functools.partial(conv_grad, q), 0)

        def narrow(n, carry):
            du_buf[chunk_rows(n, q), :] = work[n, q * CHUNK : (q + 1) * CHUNK, :].astype(BF16)
            return carry

        lax.fori_loop(0, count, narrow, 0, unroll=8)
        du_got[chunk_rows(me, q), :] = du_buf[chunk_rows(me, q), :]
        each_peer(lambda p: send(du_buf.at[chunk_rows(p, q)], du_got.at[chunk_rows(me, q)], DU + q, {"ctx": p}))
        send_some(q + 1)

    def filter_grad(q, i, carry):
        rows = rows_of(i, STEP * count)
        spec = forward(gather_rows(u_got.at[q], (i - q * steps) * STEP, count), first_two, twist, second, True)
        scatter_rows(gf_buf, i * STEP, inverse(conj_product(spec_dy[rows, :], spec), twist, third, last))
        return carry

    def filter_chunk(q):
        wait_for(recv_sem, U + q, u_got.at[q, others])
        lax.fori_loop(q * steps, (q + 1) * steps, functools.partial(filter_grad, q), 0)

    unfilled = list(range(CHUNKS))

    def fill(position):
        for _ in range(FILLS[position]):
            filter_chunk(unfilled.pop(0))

    fill(0)

    for q in range(CHUNKS):
        wait_for(recv_sem, DU + q, dy_got.at[q, others])
    r_mine[...] = dot(b_ref[...], du_got[...])
    each_group(lambda g: send(r_mine, r_got.at[grp], 1, {"grp": g}))

    blocks = width // LANES
    half = ranks * blocks

    def outer(value, tokens, offset):
        first, rest = split(value)
        both = dot(jnp.concatenate([first, rest], axis=0), tokens, ((1,), (1,)))
        out = (both[:ranks] + both[ranks:]) * factor
        for k in range(blocks):
            parts[pl.ds(offset + k, ranks, stride=blocks), :] = out[:, k * LANES : (k + 1) * LANES]

    def tile_of(p):
        return rows_of(p % 2 * (count // 2) + p // 2, 8)

    def send_parts(role):
        each_owner(role, lambda p: send(parts.at[tile_of(p)], part_got.at[me], 2, {"ctx": p}))

    outer(z, du_got[...], half)
    send_parts(1)
    wait_for(recv_sem, 1, r_got.at[pl.ds(0, groups - 1)])
    rank_grad = shared_sum(r_mine, r_got)
    outer(rank_grad, x_buf[...], 0)
    send_parts(0)
    part_got[me] = parts[tile_of(me), :]
    low_rank(lambda s, n: du_got[s : s + n, :], a_ref, rank_grad, gi_ref)

    fill(1)
    wait_for(recv_sem, 2, part_got.at[others])
    acc = jnp.sum(part_got[...], axis=0)
    total[...] = acc
    total_got[tile_of(me), :] = acc
    each_peer(lambda p: send(total, total_got.at[tile_of(me)], 3, {"ctx": p}))
    fill(2)

    def store_gf(n, carry):
        pltpu.make_async_copy(gf_buf.at[n], gf_ref.at[:, lanes_of(n)], load_sem.at[11]).start()
        return carry

    lax.fori_loop(0, count, store_gf, 0)

    wait_for(recv_sem, 3, part_got.at[others])
    gd_ref[...] = total_got[pl.ds(0, half), :]
    gu_ref[...] = total_got[pl.ds(half, half), :]

    pltpu.make_async_copy(gf_buf, gf_buf, load_sem.at[11]).wait()
    for slot in range(2):
        wait_for(send_sem, slot, z_got.at[pl.ds(0, groups - 1)])
    for slot in range(2, 4):
        wait_for(send_sem, slot, part_got.at[others])
    for slot in range(DY, DY + 3 * CHUNKS):
        wait_for(send_sem, slot, dy_got.at[0, others])


def store_kernel(gi, gf, gd, gu, gi_out, gf_out, gd_out, gu_out, sems):
    copies = [
        pltpu.make_async_copy(src, dst, sems.at[k])
        for k, (src, dst) in enumerate([(gf, gf_out), (gi, gi_out), (gd, gd_out), (gu, gu_out)])
    ]
    for copy in copies:
        copy.start()
    for copy in copies:
        copy.wait()


def body(count, groups, saved_input, out_grad, filters, adapter_down, adapter_up):
    width, tokens = saved_input.shape[1], filters.shape[2]
    ranks = adapter_down.shape[0]
    tables = [jnp.asarray(t) for t in make_tables(count)]
    rows = count * CHANS
    hbm = pl.BlockSpec(memory_space=pl.ANY)
    source = pl.BlockSpec(memory_space=SOURCE)
    spec = pltpu.VMEM((rows, 2 * LANES), F32)
    small = pltpu.VMEM((ranks, LANES), F32)
    some = pltpu.VMEM((groups, ranks, LANES), F32)
    narrow = pltpu.VMEM((rows, LANES), BF16)
    wide = pltpu.VMEM((count, CHANS, LANES), F32)
    maps = pltpu.VMEM((ranks, width), BF16)
    tiles = pltpu.VMEM((count * 8, LANES), F32)
    got = pltpu.VMEM((CHUNKS, count, CHUNK, LANES), BF16)
    flat = ranks * width // LANES
    results = pl.pallas_call(
        functools.partial(kernel, count, groups, float(tokens) ** -0.5),
        out_shape=(
            pltpu.VMEM((width, LANES), BF16),
            pltpu.VMEM((CHANS, tokens), F32),
            pltpu.VMEM((flat, LANES), F32),
            pltpu.VMEM((flat, LANES), F32),
        ),
        in_specs=[source] * 11,
        out_specs=(pl.BlockSpec(memory_space=pltpu.VMEM),) * 4,
        scratch_shapes=[
            maps, maps, *[pltpu.VMEM(t.shape, t.dtype) for t in tables],
            narrow, wide, narrow, narrow, got, got, narrow, wide, wide,
            spec, spec, small, some, small, some, tiles, pltpu.VMEM((count, 8, LANES), F32),
            pltpu.VMEM((8, LANES), F32), tiles,
            pltpu.SemaphoreType.DMA((12 + CHUNKS,)),
            pltpu.SemaphoreType.DMA((4 + 3 * CHUNKS,)),
            pltpu.SemaphoreType.DMA((4 + 3 * CHUNKS,)),
        ],
        compiler_params=pltpu.CompilerParams(
            collective_id=0, has_side_effects=True, vmem_limit_bytes=VMEM_LIMIT
        ),
    )(saved_input[0], out_grad[0], filters[0], adapter_down[:, 0, :], adapter_up[:, 0, :], *tables)
    grad_input, grad_filter, down, up = pl.pallas_call(
        store_kernel,
        out_shape=tuple(jax.ShapeDtypeStruct(r.shape, r.dtype) for r in results),
        in_specs=[pl.BlockSpec(memory_space=pltpu.VMEM)] * 4,
        out_specs=(hbm,) * 4,
        scratch_shapes=[pltpu.SemaphoreType.DMA((4,))],
    )(*[pltpu.with_memory_space_constraint(r, pltpu.VMEM) for r in results])
    return (
        grad_input[None],
        grad_filter[None],
        down.reshape(ranks, 1, width),
        up.reshape(ranks, 1, width),
    )


def solution(mesh):
    placed = (
        P("grp", None, "ctx"),
        P("grp", None, "ctx"),
        P("grp", "ctx", None),
        P(None, "grp", None),
        P(None, "grp", None),
    )
    return jax.shard_map(
        functools.partial(body, mesh.shape["ctx"], mesh.shape["grp"]),
        mesh=mesh,
        in_specs=placed,
        out_specs=(
            P("grp", None, "ctx"),
            P("grp", "ctx", None),
            P(None, "grp", None),
            P(None, "grp", None),
        ),
        check_vma=False,
    )
```

profile of v0, /device:TPU:1, one launch (start us, length us, event | category | flops | bytes accessed | tf_op | source)
XLA Modules:
  0.0 48.4 jit_solution(17425745067481202759)
XLA Ops:
  0.6 46.5 %shard_map.138 = (bf16[2048,128]{1,0:T(8,128)(2,1)S(1)}, f32[32,8192]{1,0:T(8,128)S(1)}, f32[256,128]{1,0:T(8,128)S(1)}, f32[256,128]{1,0:T(8,128)S(1)}) custom-call(bf16[2048,128]{1,0:T(8,128)(2,1)} %bitcast.10, bf16[2048,128]{1,0:T(8,128)(2,1)} %bitcast.11, f32[32,8192]{1,0:T(8,128)} %bitcast.9, bf16[16,2048]{1,0:T(8,128)(2,1)} %bitcast.12, ...), custom_call_target="tpu_custom_call" | custom-call | tf_op jit(solution)/shard_map/pallas_call | solution.py:422
  47.1 1.3 %shard_map.139 = (bf16[2048,128]{1,0:T(8,128)(2,1)}, f32[32,8192]{1,0:T(8,128)}, f32[256,128]{1,0:T(8,128)}, f32[256,128]{1,0:T(8,128)}) custom-call(bf16[2048,128]{1,0:T(8,128)(2,1)S(1)} %get-tuple-element.12.gi, f32[32,8192]{1,0:T(8,128)S(1)} %get-tuple-element.13.gf, f32[256,128]{1,0:T(8,128)S(1)} %get-tuple-element.14.gd, ...), custom_call_target="tpu_custom_call" | custom-call | tf_op jit(solution)/shard_map/pallas_call | solution.py:445
where the time goes:
time: 48.5 us; the launch traced here: 48.4 us
  Pallas kernels  47.7 us (98%)
  between operations  0.64 us (1%)
    pallas_call x1, Pallas kernels, body(): pl.pallas_call(functools.partial(kernel, count, groups, float(tokens) **...  46.5 us
    pallas_call x1, Pallas kernels, body(): pl.pallas_call(store_kernel, out_shape=tuple((jax.ShapeDtypeStruct(r.shap...  1.25 us

commit v1 on v0

--- a/solution.py
+++ b/solution.py
@@ -363,7 +363,6 @@
     outer(rank_grad, x_buf[...], 0)
     send_parts(0)
     part_got[me] = parts[tile_of(me), :]
-    low_rank(lambda s, n: du_got[s : s + n, :], a_ref, rank_grad, gi_ref)
 
     fill(1)
     wait_for(recv_sem, 2, part_got.at[others])
@@ -371,6 +370,7 @@
     total[...] = acc
     total_got[tile_of(me), :] = acc
     each_peer(lambda p: send(total, total_got.at[tile_of(me)], 3, {"ctx": p}))
+    low_rank(lambda s, n: du_got[s : s + n, :], a_ref, rank_grad, gi_ref)
     fill(2)
 
     def store_gf(n, carry):

time: 48.5 us -> 48.5 us (level)
  no operation moved by 1% of the time
where the time goes in v1:
time: 48.5 us; the launch traced here: 48.4 us
  Pallas kernels  47.8 us (99%)
  between operations  0.64 us (1%)
    pallas_call x1, Pallas kernels, body(): pl.pallas_call(functools.partial(kernel, count, groups, float(tokens) **...  46.5 us
    pallas_call x1, Pallas kernels, body(): pl.pallas_call(store_kernel, out_shape=tuple((jax.ShapeDtypeStruct(r.shap...  1.25 us

profile of v1, /device:TPU:1, one launch (start us, length us, event | category | flops | bytes accessed | tf_op | source)
XLA Modules:
  0.0 48.4 jit_solution(12201442153483088426)
XLA Ops:
  0.6 46.5 %shard_map.138 = (bf16[2048,128]{1,0:T(8,128)(2,1)S(1)}, f32[32,8192]{1,0:T(8,128)S(1)}, f32[256,128]{1,0:T(8,128)S(1)}, f32[256,128]{1,0:T(8,128)S(1)}) custom-call(bf16[2048,128]{1,0:T(8,128)(2,1)} %bitcast.10, bf16[2048,128]{1,0:T(8,128)(2,1)} %bitcast.11, f32[32,8192]{1,0:T(8,128)} %bitcast.9, bf16[16,2048]{1,0:T(8,128)(2,1)} %bitcast.12, ...), custom_call_target="tpu_custom_call" | custom-call | tf_op jit(solution)/shard_map/pallas_call | solution.py:422
  47.2 1.3 %shard_map.139 = (bf16[2048,128]{1,0:T(8,128)(2,1)}, f32[32,8192]{1,0:T(8,128)}, f32[256,128]{1,0:T(8,128)}, f32[256,128]{1,0:T(8,128)}) custom-call(bf16[2048,128]{1,0:T(8,128)(2,1)S(1)} %get-tuple-element.12.gi, f32[32,8192]{1,0:T(8,128)S(1)} %get-tuple-element.13.gf, f32[256,128]{1,0:T(8,128)S(1)} %get-tuple-element.14.gd, ...), custom_call_target="tpu_custom_call" | custom-call | tf_op jit(solution)/shard_map/pallas_call | solution.py:445
